TPU v7x, 512 devices: a whole 4x4x16 slice. The times are simulated.
512 devices in a mesh: dp: 64 (over z, y), feat: 8 (over x, core).
Axes of the slice: x: 4, y: 4, z: 16, core: 2. Of those that a mesh axis runs over, the one named last changes fastest.
Arguments:
- points: float32 [65536, 256], P('dp'), may hold values from -6 to 6
- frequencies: float32 [256, 1024], P(None, 'feat'), may hold values from -0.5 to 0.5
- halton_start: int32 [1], replicated, may hold values from 0 to 39999
Outputs:
- scores: float32 [65536], P(('dp', 'feat'))
- r_factor: float32 [1024, 1024], P(None, 'feat')
All inputs are finite; a program needn't handle non-finite values.
Results may differ from a plain program's by a relative error of at most 0.0003.
Values sent between devices are 32-bit elements; how exact they have to be, the bound alone decides.
A program may use at most 64 MiB of HBM per device.

v0:
```python
import math
import jax
import jax.numpy as jnp
from jax import lax
from jax.sharding import PartitionSpec as P

ridge_level = 0.1


def halton_phase(halton_start, columns):
    index_value = halton_start[0] + columns
    radical = jnp.zeros(columns.shape, jnp.float32)
    for place in range(16):
        digit_bit = index_value // (1 << place) % 2
        radical = radical + digit_bit.astype(jnp.float32) * 0.5 ** (place + 1)
    return 2.0 * math.pi * radical


def featurize(row_block, frequencies, phase):
    angles = jnp.dot(
        row_block, frequencies, precision=lax.Precision.HIGHEST, preferred_element_type=jnp.float32
    )
    return math.sqrt(2.0) * jnp.cos(angles + phase)


def per_device(points, frequencies, halton_start):
    panel_width = frequencies.shape[1]
    feat_count = lax.axis_size("feat")
    group_count = lax.axis_size("dp")
    feat_total = panel_width * feat_count
    row_count = points.shape[0]
    total_rows = row_count * group_count
    feat_place = lax.axis_index("feat")
    columns = feat_place * panel_width + jnp.arange(panel_width, dtype=jnp.int32)
    own_panel = featurize(points, frequencies, halton_phase(halton_start, columns))
    gram_block = jnp.dot(
        lax.all_gather(own_panel, "feat", axis=1, tiled=True).T,
        own_panel,
        precision=lax.Precision.HIGHEST,
        preferred_element_type=jnp.float32,
    )
    own_rows = lax.all_to_all(own_panel, "feat", split_axis=0, concat_axis=1, tiled=True)
    summed = lax.psum(gram_block, "dp")
    gram_total = lax.all_gather(summed, "feat", axis=1, tiled=True)
    gram_full = gram_total / total_rows + ridge_level * jnp.eye(feat_total, dtype=jnp.float32)
    factor = jnp.linalg.cholesky(gram_full)
    solved = lax.linalg.triangular_solve(factor, own_rows.T, left_side=True, lower=True)
    scores = jnp.sum(solved * solved, axis=0) / feat_total
    own_factor = lax.dynamic_slice_in_dim(factor, feat_place * panel_width, panel_width, 1)
    return (scores, own_factor)


def solution(mesh):
    in_specs = (P("dp", None), P(None, "feat"), P())
    out_specs = (P(("dp", "feat")), P(None, "feat"))
    return jax.shard_map(
        per_device, mesh=mesh, in_specs=in_specs, out_specs=out_specs, check_vma=False
    )
```

profile of v0, /device:TPU:1, one launch (start us, length us, event | category | flops | bytes accessed | tf_op | source)
XLA Modules:
  0.0 727.1 jit_solution(13208123939911550002)
XLA Ops:
  8.4 4.3 fusion.3
  12.8 49.5 %all-gather.3.cloned.1.call-done = f32[1024,1024]{1,0:T(8,128)} async-done(((f32[1024,128]{1,0:T(8,128)}), f32[1024,1024]{1,0:T(8,128)}) %all-gather.3.cloned.1.call-update) | async-done | bytes 4194320 | tf_op jit(solution)/shard_map/all_gather | solution.py:37
  62.3 5.6 fusion.128
  68.0 256.7 %all-reduce.3.cloned.1.call-done = f32[1024,128]{0,1:T(8,128)} async-done(((f32[1024,128]{0,1:T(8,128)}), f32[1024,128]{0,1:T(8,128)}) %all-reduce.3.cloned.1.call-update) | async-done | bytes 524304 | tf_op jit(solution)/shard_map/psum | solution.py:43
  325.7 15.0 %all-to-all-start = ((f32[8,128,128]{1,2,0:T(8,128)}), f32[8,128,128]{1,2,0:T(8,128)S(1)}, u32[]{:S(2)}, u32[]{:S(2)}) async-start(f32[8,128,128]{1,2,0:T(8,128)} %copy.42), calls=%async_computation | async-start | bytes 1048576 | tf_op jit(solution)/shard_map/all_to_all | solution.py:42
  340.7 31.0 %all-gather.5.cloned.1.call-done = f32[1024,1024]{0,1:T(8,128)} async-done(((f32[1024,128]{0,1:T(8,128)}), f32[1024,1024]{0,1:T(8,128)}) %all-gather.5.cloned.1.call-update) | async-done | bytes 4194320 | tf_op jit(solution)/shard_map/all_gather | solution.py:44
  371.7 5.0 select_add_fusion
  376.7 5.8 copy.25
  382.5 4.5 fusion
  388.9 11.7 %cholesky.222 = f32[128,128]{1,0:T(8,128)S(1)} custom-call(f32[128,128]{1,0:T(8,128)S(1)} %cholesky.577), custom_call_target="Cholesky" | custom-call | tf_op jit(solution)/shard_map/jit(cholesky)/cholesky | solution.py:46
  400.8 9.8 %custom-call.62 = f32[1,128,128]{1,2,0:T(8,128)S(1)} custom-call(f32[1,128,128]{2,1,0:T(8,128)S(1)} %get-tuple-element.72), custom_call_target="InvertDiagBlocksLowerTriangular" | custom-call | tf_op jit(solution)/shard_map/jit(cholesky)/cholesky | solution.py:46
  413.9 11.7 %cholesky.243 = f32[128,128]{1,0:T(8,128)S(1)} custom-call(f32[128,128]{1,0:T(8,128)S(1)} %cholesky.581), custom_call_target="Cholesky" | custom-call | tf_op jit(solution)/shard_map/jit(cholesky)/cholesky | solution.py:46
  425.9 9.8 %custom-call.63 = f32[1,128,128]{1,2,0:T(8,128)S(1)} custom-call(f32[1,128,128]{2,1,0:T(8,128)S(1)} %get-tuple-element.70), custom_call_target="InvertDiagBlocksLowerTriangular" | custom-call | tf_op jit(solution)/shard_map/jit(cholesky)/cholesky | solution.py:46
  438.8 2.4 convolution_subtract_fusion.1
  441.3 11.7 %cholesky.466 = f32[128,128]{1,0:T(8,128)S(1)} custom-call(f32[128,128]{1,0:T(8,128)S(1)} %cholesky.586), custom_call_target="Cholesky" | custom-call | tf_op jit(solution)/shard_map/jit(cholesky)/cholesky | solution.py:46
  453.7 9.8 %custom-call.64 = f32[1,128,128]{1,2,0:T(8,128)S(1)} custom-call(f32[1,128,128]{2,1,0:T(8,128)S(1)} %get-tuple-element.68), custom_call_target="InvertDiagBlocksLowerTriangular" | custom-call | tf_op jit(solution)/shard_map/jit(cholesky)/cholesky | solution.py:46
  464.8 3.3 convolution_subtract_fusion.2
  468.1 11.7 %cholesky.485 = f32[128,128]{1,0:T(8,128)S(1)} custom-call(f32[128,128]{1,0:T(8,128)S(1)} %cholesky.591), custom_call_target="Cholesky" | custom-call | tf_op jit(solution)/shard_map/jit(cholesky)/cholesky | solution.py:46
  480.6 9.8 %custom-call.65 = f32[1,128,128]{1,2,0:T(8,128)S(1)} custom-call(f32[1,128,128]{2,1,0:T(8,128)S(1)} %get-tuple-element.66), custom_call_target="InvertDiagBlocksLowerTriangular" | custom-call | tf_op jit(solution)/shard_map/jit(cholesky)/cholesky | solution.py:46
  491.6 3.2 convolution_subtract_fusion.3
  494.7 12.1 %cholesky.504 = f32[128,128]{1,0:T(8,128)S(1)} custom-call(f32[128,128]{1,0:T(8,128)S(1)} %cholesky.596), custom_call_target="Cholesky" | custom-call | tf_op jit(solution)/shard_map/jit(cholesky)/cholesky | solution.py:46
  507.6 9.8 %custom-call.66 = f32[1,128,128]{1,2,0:T(8,128)S(1)} custom-call(f32[1,128,128]{2,1,0:T(8,128)S(1)} %get-tuple-element.64), custom_call_target="InvertDiagBlocksLowerTriangular" | custom-call | tf_op jit(solution)/shard_map/jit(cholesky)/cholesky | solution.py:46
  518.6 3.2 convolution_subtract_fusion.4
  521.8 11.7 %cholesky.524 = f32[128,128]{1,0:T(8,128)S(1)} custom-call(f32[128,128]{1,0:T(8,128)S(1)} %cholesky.601), custom_call_target="Cholesky" | custom-call | tf_op jit(solution)/shard_map/jit(cholesky)/cholesky | solution.py:46
  534.3 9.8 %custom-call.67 = f32[1,128,128]{1,2,0:T(8,128)S(1)} custom-call(f32[1,128,128]{2,1,0:T(8,128)S(1)} %get-tuple-element.62), custom_call_target="InvertDiagBlocksLowerTriangular" | custom-call | tf_op jit(solution)/shard_map/jit(cholesky)/cholesky | solution.py:46
  545.1 2.9 convolution_subtract_fusion.5
  548.0 11.7 %cholesky.544 = f32[128,128]{1,0:T(8,128)S(1)} custom-call(f32[128,128]{1,0:T(8,128)S(1)} %cholesky.606), custom_call_target="Cholesky" | custom-call | tf_op jit(solution)/shard_map/jit(cholesky)/cholesky | solution.py:46
  560.5 9.8 %custom-call.68 = f32[1,128,128]{1,2,0:T(8,128)S(1)} custom-call(f32[1,128,128]{2,1,0:T(8,128)S(1)} %get-tuple-element.60), custom_call_target="InvertDiagBlocksLowerTriangular" | custom-call | tf_op jit(solution)/shard_map/jit(cholesky)/cholesky | solution.py:46
  573.4 11.7 %cholesky.562 = f32[128,128]{1,0:T(8,128)S(1)} custom-call(f32[128,128]{1,0:T(8,128)S(1)} %convolution_subtract_fusion.11), custom_call_target="Cholesky" | custom-call | tf_op jit(solution)/shard_map/jit(cholesky)/cholesky | solution.py:46
  595.7 6.6 fusion.1
  602.2 23.6 %while.1 = (s32[]{:T(128)}, f32[1024,1024]{0,1:T(8,128)}, s32[8,2]{0,1:T(2,128)S(1)}, f32[8,128,128]{2,1,0:T(8,128)S(1)}, s32[]{:T(128)}) while((s32[]{:T(128)}, f32[1024,1024]{0,1:T(8,128)}, s32[8,2]{0,1:T(2,128)S(1)}, f32[8,128,128]{2,1,0:T(8,128)S(1)}, s32[]{:T(128)}) %tuple.58), condition=%wide.while_cond, body=%wide.while_body.sunk | while | flops 2 | bytes 393329 | solution.py:47
  625.8 78.6 %custom-call.69 = f32[8,128,128]{1,2,0:T(8,128)S(1)} custom-call(f32[8,128,128]{2,1,0:T(8,128)S(1)} %get-tuple-element.9), custom_call_target="InvertDiagBlocksLowerTriangular" | custom-call | tf_op jit(solution)/shard_map/triangular_solve | solution.py:47
  (128 shorter events, 66.3 us)
Async XLA Ops:
  7.2 1.2 copy-start
  7.2 55.1 %all-gather.3.cloned.1.call-start = ((), (), s32[]{:S(2)}) async-start(), calls=%async_computation.1 | async-start | bytes 4718592 | tf_op jit(solution)/shard_map/all_gather | solution.py:37
  12.7 312.0 %copy-start.3 = (f32[1024,128]{1,0:T(8,128)S(1)}, f32[1024,128]{1,0:T(8,128)}, u32[]{:S(2)}) copy-start(f32[1024,128]{1,0:T(8,128)} %fusion.3) | copy-start | bytes 1572868
  12.7 312.0 %all-reduce.3.cloned.1.call-start = ((), (), s32[]{:S(2)}) async-start(), calls=%async_computation.2 | async-start | bytes 1048576 | tf_op jit(solution)/shard_map/psum | solution.py:43
  68.0 303.7 %all-gather.5.cloned.1.call-start = ((), (), s32[]{:S(2)}) async-start(), calls=%async_computation.3 | async-start | bytes 4718592 | tf_op jit(solution)/shard_map/all_gather | solution.py:44
  325.7 378.7 %all-to-all-start = ((f32[8,128,128]{1,2,0:T(8,128)}), f32[8,128,128]{1,2,0:T(8,128)S(1)}, u32[]{:S(2)}, u32[]{:S(2)}) async-start(f32[8,128,128]{1,2,0:T(8,128)} %copy.42), calls=%async_computation | async-start | bytes 1048576 | tf_op jit(solution)/shard_map/all_to_all | solution.py:42
  387.0 1.9 copy-start.2
  436.8 2.0 copy-start.1
Sparse Core Ops, SparseCore 0:
  12.8 49.4 all-gather.2
  68.1 256.5 all-reduce.2
  327.1 44.5 all-gather.4
where the time goes:
time: 733 us; the launch traced here: 727 us
  waiting for transfers between devices  337 us (46%)
  other arithmetic  263 us (36%)
  matrix products  49.2 us (7%)
  local copies, waits for them, and re-layouts  41.8 us (6%)
  between operations  20.1 us (3%)
  starting transfers between devices  15.1 us (2%)
    psum x1, waiting for transfers between devices, per_device(): summed = lax.psum(gram_block, 'dp')  257 us
    another operation x30, other arithmetic, per_device(): factor = jnp.linalg.cholesky(gram_full)  168 us
    another operation x3, other arithmetic, per_device(): lax.linalg.triangular_solve(factor, own_rows.T, left_side=True, lower=True)  85.2 us
    all_gather x1, waiting for transfers between devices, per_device(): lax.all_gather(own_panel, 'feat', axis=1, tiled=True)  49.5 us
    all_gather x1, waiting for transfers between devices, per_device(): gram_total = lax.all_gather(summed, 'feat', axis=1, tiled=True)  31 us
    another operation x14, matrix products, per_device(): factor = jnp.linalg.cholesky(gram_full)  26.2 us
    another operation x40, local copies, waits for them, and re-layouts  23.1 us
    all_to_all x1, starting transfers between devices, per_device(): lax.all_to_all(own_panel, 'feat', split_axis=0, concat_axis=1, tiled=True)  15 us
  transfers between devices with their start and end apart: 4, of which 3 were waited for; matrix products, arithmetic and copies ran while one was open for 45% of the time, Pallas kernels for 0%

commit v1 on v0

--- a/solution.py
+++ b/solution.py
@@ -40,7 +40,7 @@
         preferred_element_type=jnp.float32,
     )
     own_rows = lax.all_to_all(own_panel, "feat", split_axis=0, concat_axis=1, tiled=True)
-    summed = lax.psum(gram_block, "dp")
+    summed = jnp.sum(lax.all_gather(gram_block, "dp"), axis=0)
     gram_total = lax.all_gather(summed, "feat", axis=1, tiled=True)
     gram_full = gram_total / total_rows + ridge_level * jnp.eye(feat_total, dtype=jnp.float32)
     factor = jnp.linalg.cholesky(gram_full)

time: 733 us -> 783 us (1.068)
  waiting for transfers between devices: 337 us -> 375 us
  other arithmetic: 263 us -> 275 us
  starting transfers between devices: 15.1 us -> 5.45 us
    all_gather x0 -> x1, waiting for transfers between devices: none -> 295 us  [per_device(): summed = jnp.sum(lax.all_gather(gram_block, 'dp'), axis=0)]
    psum x1 -> x0, waiting for transfers between devices: 257 us -> none  [per_device(): summed = lax.psum(gram_block, 'dp')]
    reduce_sum x0 -> x1, other arithmetic: none -> 11.7 us  [per_device(): summed = jnp.sum(lax.all_gather(gram_block, 'dp'), axis=0)]
    all_to_all x1, starting transfers between devices: 15 us -> 5.33 us  [per_device(): lax.all_to_all(own_panel, 'feat', split_axis=0, concat_axis=1, tiled=True)]
  transfers between devices with their start and end apart: 4 -> 4, of which waited for: 3 -> 3; matrix products, arithmetic and copies ran while one was open for 45% -> 42% of each run, Pallas kernels for 0% -> 0%
where the time goes in v1:
time: 783 us; the launch traced here: 775 us
  waiting for transfers between devices  375 us (48%)
  other arithmetic  275 us (35%)
  matrix products  54.4 us (7%)
  local copies, waits for them, and re-layouts  44.3 us (6%)
  between operations  20.1 us (3%)
    all_gather x1, waiting for transfers between devices, per_device(): summed = jnp.sum(lax.all_gather(gram_block, 'dp'), axis=0)  295 us
    another operation x30, other arithmetic, per_device(): factor = jnp.linalg.cholesky(gram_full)  168 us
    another operation x3, other arithmetic, per_device(): lax.linalg.triangular_solve(factor, own_rows.T, left_side=True, lower=True)  85.2 us
    all_gather x1, waiting for transfers between devices, per_device(): lax.all_gather(own_panel, 'feat', axis=1, tiled=True)  49.5 us
    all_gather x1, waiting for transfers between devices, per_device(): gram_total = lax.all_gather(summed, 'feat', axis=1, tiled=True)  30.8 us
    another operation x14, matrix products, per_device(): factor = jnp.linalg.cholesky(gram_full)  27.3 us
    another operation x40, local copies, waits for them, and re-layouts  23.1 us
  transfers between devices with their start and end apart: 4, of which 3 were waited for; matrix products, arithmetic and copies ran while one was open for 42% of the time, Pallas kernels for 0%

profile of v1, /device:TPU:1, one launch (start us, length us, event | category | flops | bytes accessed | tf_op | source)
XLA Modules:
  0.0 774.8 jit_solution(11647475211474520326)
XLA Ops:
  8.4 4.3 fusion.3
  12.8 49.5 %all-gather.5.cloned.1.call-done = f32[1024,1024]{1,0:T(8,128)} async-done(((f32[1024,128]{1,0:T(8,128)}), f32[1024,1024]{1,0:T(8,128)}) %all-gather.5.cloned.1.call-update) | async-done | bytes 4194320 | tf_op jit(solution)/shard_map/all_gather | solution.py:37
  62.3 9.8 %fusion.128 = f32[1024,128]{1,0:T(8,128)} fusion(f32[1024,1024]{1,0:T(8,128)} %all-gather.5.cloned.1.call-done, f32[1024,128]{1,0:T(8,128)} %fusion.3), kind=kOutput, calls=%fused_computation.320 | convolution fusion | flops 1610612736 | bytes 5242880 | tf_op jit(solution)/shard_map/dot_general | solution.py:36
  72.1 294.8 %all-gather.9.cloned.1.call-done = f32[65536,128]{1,0:T(8,128)} async-done(((f32[1024,128]{1,0:T(8,128)}), f32[65536,128]{1,0:T(8,128)}) %all-gather.9.cloned.1.call-update) | async-done | bytes 33554448 | tf_op jit(solution)/shard_map/all_gather | solution.py:43
  366.9 11.7 %reduce_sum.18 = f32[1024,128]{1,0:T(8,128)S(1)} reduce(f32[64,1024,128]{2,1,0:T(8,128)} %bitcast.112, f32[]{:T(128)} %constant.572.clone.1), dimensions={0}, to_apply=%region_0.1 | reduce | flops 8257536 | bytes 34078724 | tf_op jit(solution)/shard_map/reduce_sum | solution.py:43
  380.7 5.3 all-to-all-start
  386.0 30.8 %all-gather.7.cloned.1.call-done = f32[1024,1024]{0,1:T(8,128)} async-done(((f32[1024,128]{0,1:T(8,128)}), f32[1024,1024]{0,1:T(8,128)}) %all-gather.7.cloned.1.call-update) | async-done | bytes 4194320 | tf_op jit(solution)/shard_map/all_gather | solution.py:44
  416.8 5.0 select_add_fusion
  421.8 5.8 copy.43
  427.6 4.5 fusion
  434.0 11.7 %cholesky.222 = f32[128,128]{1,0:T(8,128)S(1)} custom-call(f32[128,128]{1,0:T(8,128)S(1)} %cholesky.577), custom_call_target="Cholesky" | custom-call | tf_op jit(solution)/shard_map/jit(cholesky)/cholesky | solution.py:46
  445.8 9.8 %custom-call.62 = f32[1,128,128]{1,2,0:T(8,128)S(1)} custom-call(f32[1,128,128]{2,1,0:T(8,128)S(1)} %get-tuple-element.78), custom_call_target="InvertDiagBlocksLowerTriangular" | custom-call | tf_op jit(solution)/shard_map/jit(cholesky)/cholesky | solution.py:46
  458.7 11.7 %cholesky.243 = f32[128,128]{1,0:T(8,128)S(1)} custom-call(f32[128,128]{1,0:T(8,128)S(1)} %cholesky.581), custom_call_target="Cholesky" | custom-call | tf_op jit(solution)/shard_map/jit(cholesky)/cholesky | solution.py:46
  473.5 9.8 %custom-call.63 = f32[1,128,128]{1,2,0:T(8,128)S(1)} custom-call(f32[1,128,128]{2,1,0:T(8,128)S(1)} %get-tuple-element.76), custom_call_target="InvertDiagBlocksLowerTriangular" | custom-call | tf_op jit(solution)/shard_map/jit(cholesky)/cholesky | solution.py:46
  488.9 11.7 %cholesky.466 = f32[128,128]{1,0:T(8,128)S(1)} custom-call(f32[128,128]{1,0:T(8,128)S(1)} %cholesky.586), custom_call_target="Cholesky" | custom-call | tf_op jit(solution)/shard_map/jit(cholesky)/cholesky | solution.py:46
  501.4 9.8 %custom-call.64 = f32[1,128,128]{1,2,0:T(8,128)S(1)} custom-call(f32[1,128,128]{2,1,0:T(8,128)S(1)} %get-tuple-element.74), custom_call_target="InvertDiagBlocksLowerTriangular" | custom-call | tf_op jit(solution)/shard_map/jit(cholesky)/cholesky | solution.py:46
  512.4 3.3 convolution_subtract_fusion.2
  515.8 11.7 %cholesky.485 = f32[128,128]{1,0:T(8,128)S(1)} custom-call(f32[128,128]{1,0:T(8,128)S(1)} %cholesky.591), custom_call_target="Cholesky" | custom-call | tf_op jit(solution)/shard_map/jit(cholesky)/cholesky | solution.py:46
  528.3 9.8 %custom-call.65 = f32[1,128,128]{1,2,0:T(8,128)S(1)} custom-call(f32[1,128,128]{2,1,0:T(8,128)S(1)} %get-tuple-element.72), custom_call_target="InvertDiagBlocksLowerTriangular" | custom-call | tf_op jit(solution)/shard_map/jit(cholesky)/cholesky | solution.py:46
  539.2 3.2 convolution_subtract_fusion.3
  542.4 12.1 %cholesky.504 = f32[128,128]{1,0:T(8,128)S(1)} custom-call(f32[128,128]{1,0:T(8,128)S(1)} %cholesky.596), custom_call_target="Cholesky" | custom-call | tf_op jit(solution)/shard_map/jit(cholesky)/cholesky | solution.py:46
  555.2 9.8 %custom-call.66 = f32[1,128,128]{1,2,0:T(8,128)S(1)} custom-call(f32[1,128,128]{2,1,0:T(8,128)S(1)} %get-tuple-element.70), custom_call_target="InvertDiagBlocksLowerTriangular" | custom-call | tf_op jit(solution)/shard_map/jit(cholesky)/cholesky | solution.py:46
  566.2 3.2 convolution_subtract_fusion.4
  569.4 11.7 %cholesky.524 = f32[128,128]{1,0:T(8,128)S(1)} custom-call(f32[128,128]{1,0:T(8,128)S(1)} %cholesky.601), custom_call_target="Cholesky" | custom-call | tf_op jit(solution)/shard_map/jit(cholesky)/cholesky | solution.py:46
  581.9 9.8 %custom-call.67 = f32[1,128,128]{1,2,0:T(8,128)S(1)} custom-call(f32[1,128,128]{2,1,0:T(8,128)S(1)} %get-tuple-element.68), custom_call_target="InvertDiagBlocksLowerTriangular" | custom-call | tf_op jit(solution)/shard_map/jit(cholesky)/cholesky | solution.py:46
  592.7 2.9 convolution_subtract_fusion.5
  595.6 11.7 %cholesky.544 = f32[128,128]{1,0:T(8,128)S(1)} custom-call(f32[128,128]{1,0:T(8,128)S(1)} %cholesky.606), custom_call_target="Cholesky" | custom-call | tf_op jit(solution)/shard_map/jit(cholesky)/cholesky | solution.py:46
  608.1 9.8 %custom-call.68 = f32[1,128,128]{1,2,0:T(8,128)S(1)} custom-call(f32[1,128,128]{2,1,0:T(8,128)S(1)} %get-tuple-element.66), custom_call_target="InvertDiagBlocksLowerTriangular" | custom-call | tf_op jit(solution)/shard_map/jit(cholesky)/cholesky | solution.py:46
  621.0 11.7 %cholesky.562 = f32[128,128]{1,0:T(8,128)S(1)} custom-call(f32[128,128]{1,0:T(8,128)S(1)} %convolution_subtract_fusion.11), custom_call_target="Cholesky" | custom-call | tf_op jit(solution)/shard_map/jit(cholesky)/cholesky | solution.py:46
  643.3 6.6 fusion.1
  649.8 23.6 %while.1 = (s32[]{:T(128)}, f32[1024,1024]{0,1:T(8,128)}, s32[8,2]{0,1:T(2,128)S(1)}, f32[8,128,128]{2,1,0:T(8,128)S(1)}, s32[]{:T(128)}) while((s32[]{:T(128)}, f32[1024,1024]{0,1:T(8,128)}, s32[8,2]{0,1:T(2,128)S(1)}, f32[8,128,128]{2,1,0:T(8,128)S(1)}, s32[]{:T(128)}) %tuple.60), condition=%wide.while_cond, body=%wide.while_body.sunk | while | flops 2 | bytes 393321 | solution.py:47
  673.4 78.6 %custom-call.69 = f32[8,128,128]{1,2,0:T(8,128)S(1)} custom-call(f32[8,128,128]{2,1,0:T(8,128)S(1)} %get-tuple-element.9), custom_call_target="InvertDiagBlocksLowerTriangular" | custom-call | tf_op jit(solution)/shard_map/triangular_solve | solution.py:47
  (130 shorter events, 72.3 us)
Async XLA Ops:
  7.2 1.2 copy-start
  7.2 55.1 %all-gather.5.cloned.1.call-start = ((), (), s32[]{:S(2)}) async-start(), calls=%async_computation.1 | async-start | bytes 4718592 | tf_op jit(solution)/shard_map/all_gather | solution.py:37
  12.7 354.2 %all-gather.9.cloned.1.call-start = ((), (), s32[]{:S(2)}) async-start(), calls=%async_computation.3 | async-start | bytes 34078720 | tf_op jit(solution)/shard_map/all_gather | solution.py:43
  72.1 344.7 %all-gather.7.cloned.1.call-start = ((), (), s32[]{:S(2)}) async-start(), calls=%async_computation.2 | async-start | bytes 4718592 | tf_op jit(solution)/shard_map/all_gather | solution.py:44
  366.9 12.8 %copy-start.3 = (f32[1024,128]{1,0:T(8,128)S(1)}, f32[1024,128]{1,0:T(8,128)}, u32[]{:S(2)}) copy-start(f32[1024,128]{1,0:T(8,128)} %fusion.3) | copy-start | bytes 1572868
  380.7 371.3 %all-to-all-start = ((f32[8,128,128]{1,2,0:T(8,128)}), f32[8,128,128]{1,2,0:T(8,128)S(1)}, u32[]{:S(2)}, u32[]{:S(2)}) async-start(f32[8,128,128]{1,2,0:T(8,128)} %copy.60), calls=%async_computation | async-start | bytes 1048576 | tf_op jit(solution)/shard_map/all_to_all | solution.py:42
  432.1 1.9 copy-start.2
  755.0 13.0 %copy-start.1 = (f32[1024,256]{1,0:T(8,128)S(1)}, f32[1024,256]{1,0:T(8,128)}, u32[]{:S(2)}) copy-start(f32[1024,256]{1,0:T(8,128)} %param.3) | copy-start | bytes 3145732
Sparse Core Ops, SparseCore 0:
  12.8 49.4 all-gather.4
  72.2 294.6 all-gather.8
  379.8 36.9 all-gather.6
